TPU v7x, 32 devices: a whole 2x2x4 slice. The times are simulated.
32 devices in a mesh: clip: 8 (over z, x), row: 4 (over y, core).
Axes of the slice: x: 2, y: 2, z: 4, core: 2. Of those that a mesh axis runs over, the one named last changes fastest.
Arguments:
- features: bfloat16 [8, 128, 32, 256], P('clip', None, 'row'), may hold values from -6 to 6
- out_weight: bfloat16 [3, 128, 3, 3], replicated, may hold values from -0.1875 to 0.1875
- out_bias: float32 [3], replicated, may hold values from -0.5 to 0.5
- targets: bfloat16 [8, 3, 32, 256], P('clip', None, 'row'), may hold values from -1 to 1
- weight_one: bfloat16 [64, 3, 3, 3], replicated, may hold values from -1.25 to 1.25
- bias_one: float32 [64], replicated, may hold values from -0.2 to 0.2
- weight_two: bfloat16 [64, 64, 3, 3], replicated, may hold values from -0.375 to 0.375
- bias_two: float32 [64], replicated, may hold values from -0.2 to 0.2
- weight_three: bfloat16 [128, 64, 3, 3], replicated, may hold values from -0.375 to 0.375
- bias_three: float32 [128], replicated, may hold values from -0.2 to 0.2
- weight_four: bfloat16 [128, 128, 3, 3], replicated, may hold values from -0.25 to 0.25
- bias_four: float32 [128], replicated, may hold values from -0.2 to 0.2
- lin_one: float32 [64], replicated, may hold values from 0.05 to 0.5
- lin_two: float32 [128], replicated, may hold values from 0.05 to 0.5
Outputs:
- loss: float32 [], replicated
- feature_grad: bfloat16 [8, 128, 32, 256], P('clip', None, 'row')
- out_weight_grad: float32 [3, 128, 3, 3], replicated
- out_bias_grad: float32 [3], replicated
All inputs are finite; a program needn't handle non-finite values.
Results may differ from a plain program's by a relative error of at most 0.02.
Values may be sent and summed in bfloat16 or wider, within the bound.
A program may use at most 64 MiB of HBM per device.

v0:
```python
import math

import jax
import jax.numpy as jnp
from jax import lax
from jax.sharding import PartitionSpec as P

shift_values = [-0.03, -0.088, -0.188]
scale_values = [0.458, 0.448, 0.45]


def padded_2(array, sides, width):
    for axis, dim in sides:
        size, length = (lax.axis_size(axis), array.shape[dim])
        up = [(i, (i + 1) % size) for i in range(size - 1)]
        down = [(j, i) for i, j in up]
        last = lax.slice_in_dim(array, length - width, length, axis=dim)
        leading = lax.slice_in_dim(array, 0, width, axis=dim)
        before = lax.ppermute(last, axis, up)
        after = lax.ppermute(leading, axis, down)
        array = jnp.concatenate([before, array, after], axis=dim)
    return array


def shifted(array, axis, by):
    size = lax.axis_size(axis)
    pairs = [(i, i + by) for i in range(size) if 0 <= i + by < size]
    return lax.ppermute(array, axis, pairs)


def shift_array():
    return jnp.array(shift_values, jnp.float32).reshape(1, 3, 1, 1)


def scale_array():
    return jnp.array(scale_values, jnp.float32).reshape(1, 3, 1, 1)


def gelu_exact(values):
    return values * 0.5 * (1.0 + jax.scipy.special.erf(values / math.sqrt(2.0)))


def gelu_slope(values):
    normal_cdf = 0.5 * (1.0 + jax.scipy.special.erf(values / math.sqrt(2.0)))
    density = jnp.exp(-0.5 * values * values) / math.sqrt(2.0 * math.pi)
    return normal_cdf + values * density


def pad_rows(inputs):
    return jnp.pad(inputs, ((0, 0), (0, 0), (1, 1), (0, 0)))


def flipped(weight):
    return jnp.flip(weight, (2, 3)).transpose(1, 0, 2, 3)


def conv_valid(padded, weight):
    frame_count, channels, row_total, col_count = padded.shape
    row_count = row_total - 2
    outputs = weight.shape[0]
    wide = jnp.pad(padded, ((0, 0), (0, 0), (0, 0), (1, 1)))
    total = jnp.zeros((outputs, row_count * col_count), jnp.float32)
    for row_shift in range(3):
        for col_shift in range(3):
            piece = wide[0, :, row_shift : row_shift + row_count, col_shift : col_shift + col_count]
            total = total + jnp.dot(
                weight[:, :, row_shift, col_shift],
                piece.reshape(channels, row_count * col_count),
                preferred_element_type=jnp.float32,
            )
    results = [total.reshape(outputs, row_count, col_count)]
    return jnp.stack(results)


def grad_from_output(inputs, grad_pad):
    frame_count, channels, row_count, col_count = inputs.shape
    outputs = grad_pad.shape[1]
    wide = jnp.pad(grad_pad, ((0, 0), (0, 0), (0, 0), (1, 1)))
    blocks = []
    for row_shift in range(3):
        for col_shift in range(3):
            left = wide[
                0,
                :,
                2 - row_shift : 2 - row_shift + row_count,
                2 - col_shift : 2 - col_shift + col_count,
            ].reshape(outputs, row_count * col_count)
            right = inputs[0].reshape(channels, row_count * col_count)
            total = lax.dot_general(
                left, right, (((1,), (1,)), ((), ())), preferred_element_type=jnp.float32
            )
            blocks.append(total)
    return jnp.stack(blocks).reshape(3, 3, outputs, channels).transpose(2, 3, 0, 1)


def edge_terms(row_values, kernel_row):
    col_count = row_values.shape[2]
    wide = jnp.pad(row_values, ((0, 0), (0, 0), (1, 1)))
    total = jnp.zeros((row_values.shape[0], kernel_row.shape[0], col_count), jnp.float32)
    for col_shift in range(3):
        total = total + jnp.einsum(
            "oc,fcw->fow",
            kernel_row[:, :, col_shift],
            wide[:, :, col_shift : col_shift + col_count],
            preferred_element_type=jnp.float32,
        )
    return total


def pool_mean(values):
    frame_count, channels, row_count, col_count = values.shape
    return values.reshape(frame_count, channels, row_count // 2, 2, col_count // 2, 2).mean(
        axis=(3, 5)
    )


def upsample(values):
    return jnp.repeat(jnp.repeat(values, 2, 2), 2, 3)


def vgg_forward(image, weights):
    weight_one, bias_one, weight_two, bias_two, weight_three, bias_three, weight_four, bias_four = (
        weights
    )
    image_pad = padded_2(image, (("row", 2),), 1)
    pre_one = conv_valid(image_pad, weight_one) + bias_one[None, :, None, None]
    act_one = gelu_exact(pre_one).astype(jnp.bfloat16)
    act_pad = padded_2(act_one, (("row", 2),), 1)
    pre_two = conv_valid(act_pad, weight_two) + bias_two[None, :, None, None]
    act_two = gelu_exact(pre_two)
    pooled = pool_mean(act_two).astype(jnp.bfloat16)
    pooled_pad = padded_2(pooled, (("row", 2),), 1)
    pre_three = conv_valid(pooled_pad, weight_three) + bias_three[None, :, None, None]
    act_three = gelu_exact(pre_three).astype(jnp.bfloat16)
    three_pad = padded_2(act_three, (("row", 2),), 1)
    pre_four = conv_valid(three_pad, weight_four) + bias_four[None, :, None, None]
    act_four = gelu_exact(pre_four)
    return (pre_one, pre_two, act_two, pre_three, pre_four, act_four)


def lpips_layer(feat_dec, feat_tgt, lin, count):
    norm_dec = jnp.sqrt(jnp.sum(feat_dec * feat_dec, 1, keepdims=True) + 1e-06)
    norm_tgt = jnp.sqrt(jnp.sum(feat_tgt * feat_tgt, 1, keepdims=True) + 1e-06)
    unit_dec = feat_dec / norm_dec
    differ = unit_dec - feat_tgt / norm_tgt
    scaled = lin[None, :, None, None]
    part = jnp.sum(scaled * differ * differ) / count
    grad_unit = 2.0 * scaled * differ / count
    grad_feat = (grad_unit - unit_dec * jnp.sum(grad_unit * unit_dec, 1, keepdims=True)) / norm_dec
    return (part, grad_feat)


def local(
    features,
    out_weight,
    out_bias,
    targets,
    weight_one,
    bias_one,
    weight_two,
    bias_two,
    weight_three,
    bias_three,
    weight_four,
    bias_four,
    lin_one,
    lin_two,
):
    weights = (
        weight_one,
        bias_one,
        weight_two,
        bias_two,
        weight_three,
        bias_three,
        weight_four,
        bias_four,
    )
    row_count = features.shape[2]
    width = features.shape[3]
    height = row_count * lax.axis_size("row")
    pre_out = conv_valid(pad_rows(features), out_weight)
    down_terms = edge_terms(features[:, :, row_count - 1, :], out_weight[:, :, 0, :])
    up_terms = edge_terms(features[:, :, 0, :], out_weight[:, :, 2, :])
    from_above = shifted(down_terms, "row", 1)
    from_below = shifted(up_terms, "row", -1)
    pre_out = pre_out.at[:, :, 0, :].add(from_above)
    pre_out = pre_out.at[:, :, row_count - 1, :].add(from_below)
    decoded = (pre_out + out_bias[None, :, None, None]).astype(jnp.bfloat16)
    image_dec = ((decoded.astype(jnp.float32) - shift_array()) / scale_array()).astype(jnp.bfloat16)
    image_tgt = ((targets.astype(jnp.float32) - shift_array()) / scale_array()).astype(jnp.bfloat16)
    pre_one, pre_two, act_two, pre_three, pre_four, act_four = vgg_forward(image_dec, weights)
    tgt_acts = vgg_forward(image_tgt, weights)
    part_one, grad_two = lpips_layer(act_two, tgt_acts[2], lin_one, float(height * width))
    part_two, grad_four = lpips_layer(
        act_four, tgt_acts[5], lin_two, float(height // 2 * (width // 2))
    )
    grad_pre4 = (grad_four * gelu_slope(pre_four)).astype(jnp.bfloat16)
    grad_act3 = conv_valid(padded_2(grad_pre4, (("row", 2),), 1), flipped(weight_four))
    grad_pre3 = (grad_act3 * gelu_slope(pre_three)).astype(jnp.bfloat16)
    grad_pool = conv_valid(padded_2(grad_pre3, (("row", 2),), 1), flipped(weight_three))
    grad_pre2 = ((grad_two + 0.25 * upsample(grad_pool)) * gelu_slope(pre_two)).astype(jnp.bfloat16)
    grad_act1 = conv_valid(padded_2(grad_pre2, (("row", 2),), 1), flipped(weight_two))
    grad_pre1 = (grad_act1 * gelu_slope(pre_one)).astype(jnp.bfloat16)
    grad_image = conv_valid(padded_2(grad_pre1, (("row", 2),), 1), flipped(weight_one))
    grad_dec = (grad_image / scale_array()).astype(jnp.bfloat16)
    grad_pad = padded_2(grad_dec, (("row", 2),), 1)
    feature_grad = conv_valid(grad_pad, flipped(out_weight)).astype(jnp.bfloat16)
    weight_grad = grad_from_output(features, grad_pad)
    bias_grad = jnp.sum(grad_dec.astype(jnp.float32), (0, 2, 3))
    loss, weight_total, bias_total = lax.psum(
        (part_one + part_two, weight_grad, bias_grad), ("clip", "row")
    )
    return (loss, feature_grad, weight_total, bias_total)


def solution(mesh):
    placed = (
        P("clip", None, "row", None),
        P(),
        P(),
        P("clip", None, "row", None),
        P(),
        P(),
        P(),
        P(),
        P(),
        P(),
        P(),
        P(),
        P(),
        P(),
    )
    return jax.shard_map(
        local,
        mesh=mesh,
        in_specs=placed,
        out_specs=(P(), P("clip", None, "row", None), P(), P()),
        check_vma=False,
    )
```

profile of v0, /device:TPU:0, one launch (start us, length us, event | category | flops | bytes accessed | tf_op | source)
XLA Modules:
  0.0 208.2 jit_solution(6531382458531928736)
XLA Ops:
  0.7 0.8 slice_bitcast_fusion.54
  1.4 1.4 fusion.406
  3.4 2.4 %collective-permute-start = (f32[1,3,256]{2,1,0:T(4,128)S(1)}, f32[1,3,256]{2,1,0:T(4,128)S(1)}, u32[]{:S(2)}, u32[]{:S(2)}) collective-permute-start(f32[1,3,256]{2,1,0:T(4,128)S(1)} %fusion.18), channel_id=1, source_target_pairs={{0,1},{1,2},{2,3},{4,5},{5,6},{6,7},{8,9},{9,10},{10,11},{12,13},{... | collective-permute-start | bytes 9224 | tf_op jit(solution)/shard_map/ppermute | solution.py:28
  6.4 1.3 collective-permute-start.1
  8.3 1.4 pad_slice_fusion
  11.3 0.5 broadcast_multiply_fusion
  11.8 0.8 reverse_bitcast_fusion
  14.9 0.7 reverse_bitcast_fusion.2
  15.8 5.2 %collective-permute-start.2 = (bf16[1,3,1,256]{3,1,2,0:T(4,128)(2,1)S(1)}, bf16[1,3,1,256]{3,1,2,0:T(4,128)(2,1)S(1)}, u32[]{:S(2)}, u32[]{:S(2)}) collective-permute-start(bf16[1,3,1,256]{3,1,2,0:T(4,128)(2,1)S(1)} %get-tuple-element.202), channel_id=1, source_target_pairs={{0,1},{1,2},{2,3},{4,5},{5,6},{6,7},{8,9},{9,10},{10,11},{12,13},{... | collective-permute-start | bytes 4616 | tf_op jit(solution)/shard_map/ppermute | solution.py:19
  20.9 1.3 collective-permute-start.3
  22.2 4.3 %collective-permute-start.6 = (bf16[1,3,1,256]{3,1,2,0:T(4,128)(2,1)S(1)}, bf16[1,3,1,256]{3,1,2,0:T(4,128)(2,1)S(1)}, u32[]{:S(2)}, u32[]{:S(2)}) collective-permute-start(bf16[1,3,1,256]{3,1,2,0:T(4,128)(2,1)S(1)} %get-tuple-element.198), channel_id=1, source_target_pairs={{0,1},{1,2},{2,3},{4,5},{5,6},{6,7},{8,9},{9,10},{10,11},{12,13},{... | collective-permute-start | bytes 4616 | tf_op jit(solution)/shard_map/ppermute | solution.py:19
  26.5 1.3 collective-permute-start.7
  34.3 4.3 %collective-permute-start.8 = (bf16[1,64,1,256]{3,2,1,0:T(2,128)(2,1)S(1)}, bf16[1,64,1,256]{3,2,1,0:T(2,128)(2,1)S(1)}, u32[]{:S(2)}, u32[]{:S(2)}) collective-permute-start(bf16[1,64,1,256]{3,2,1,0:T(2,128)(2,1)S(1)} %get-tuple-element.108), channel_id=1, source_target_pairs={{0,1},{1,2},{2,3},{4,5},{5,6},{6,7},{8,9},{9,10},{10,11},{12,13},{... | collective-permute-start | bytes 98312 | tf_op jit(solution)/shard_map/ppermute | solution.py:19
  38.5 1.3 collective-permute-start.9
  40.1 4.2 %collective-permute-start.4 = (bf16[1,64,1,256]{3,2,1,0:T(2,128)(2,1)S(1)}, bf16[1,64,1,256]{3,2,1,0:T(2,128)(2,1)S(1)}, u32[]{:S(2)}, u32[]{:S(2)}) collective-permute-start(bf16[1,64,1,256]{3,2,1,0:T(2,128)(2,1)S(1)} %get-tuple-element.112), channel_id=1, source_target_pairs={{0,1},{1,2},{2,3},{4,5},{5,6},{6,7},{8,9},{9,10},{10,11},{12,13},{... | collective-permute-start | bytes 98312 | tf_op jit(solution)/shard_map/ppermute | solution.py:19
  44.3 1.5 collective-permute-start.5
  46.1 2.5 %collective-permute-done.5 = bf16[1,64,1,256]{3,2,1,0:T(2,128)(2,1)S(1)} collective-permute-done((bf16[1,64,1,256]{3,2,1,0:T(2,128)(2,1)S(1)}, bf16[1,64,1,256]{3,2,1,0:T(2,128)(2,1)S(1)}, u32[]{:S(2)}, u32[]{:S(2)}) %collective-permute-start.5) | collective-permute-done | bytes 32800 | tf_op jit(solution)/shard_map/ppermute | solution.py:20
  49.5 0.8 copy-done.6
  55.1 1.2 multiply_reduce_fusion.3
  56.4 1.3 copy.255
  57.6 1.4 copy.256
  59.1 1.3 copy.252
  60.3 2.1 %copy.253 = f32[1,64,4,2,128,2]{4,1,5,3,2,0:T(8,128)} copy(f32[1,64,4,2,128,2]{1,5,4,3,2,0:T(2,128)} %bitcast.1069) | data formatting | bytes 1048576 | tf_op jit(solution)/shard_map/stack;reshape | solution.py:72
  62.5 2.1 multiply_reduce_fusion.2
  64.5 1.1 copy.350
  65.6 0.7 multiply_convert_fusion.8
  66.5 4.8 %collective-permute-start.14 = (bf16[1,64,1,128]{1,3,2,0:T(8,128)(2,1)S(1)}, bf16[1,64,1,128]{1,3,2,0:T(8,128)(2,1)S(1)}, u32[]{:S(2)}, u32[]{:S(2)}) collective-permute-start(bf16[1,64,1,128]{1,3,2,0:T(8,128)(2,1)S(1)} %get-tuple-element.172), channel_id=1, source_target_pairs={{0,1},{1,2},{2,3},{4,5},{5,6},{6,7},{8,9},{9,10},{10,11},{12,13},{... | collective-permute-start | bytes 49160 | tf_op jit(solution)/shard_map/ppermute | solution.py:19
  71.4 1.4 collective-permute-start.15
  72.8 3.0 %collective-permute-start.10 = (bf16[1,64,1,128]{1,3,2,0:T(8,128)(2,1)S(1)}, bf16[1,64,1,128]{1,3,2,0:T(8,128)(2,1)S(1)}, u32[]{:S(2)}, u32[]{:S(2)}) collective-permute-start(bf16[1,64,1,128]{1,3,2,0:T(8,128)(2,1)S(1)} %get-tuple-element.164), channel_id=1, source_target_pairs={{0,1},{1,2},{2,3},{4,5},{5,6},{6,7},{8,9},{9,10},{10,11},{12,13},{... | collective-permute-start | bytes 49160 | tf_op jit(solution)/shard_map/ppermute | solution.py:19
  75.9 1.3 collective-permute-start.11
  77.8 2.0 collective-permute-done.11
  83.6 4.5 %collective-permute-start.16 = (bf16[1,128,1,128]{1,3,2,0:T(8,128)(2,1)S(1)}, bf16[1,128,1,128]{1,3,2,0:T(8,128)(2,1)S(1)}, u32[]{:S(2)}, u32[]{:S(2)}) collective-permute-start(bf16[1,128,1,128]{1,3,2,0:T(8,128)(2,1)S(1)} %get-tuple-element.168), channel_id=1, source_target_pairs={{0,1},{1,2},{2,3},{4,5},{5,6},{6,7},{8,9},{9,10},{10,11},{12,13},{... | collective-permute-start | bytes 98312 | tf_op jit(solution)/shard_map/ppermute | solution.py:19
  88.1 1.3 collective-permute-start.17
  89.5 3.0 %collective-permute-start.12 = (bf16[1,128,1,128]{1,3,2,0:T(8,128)(2,1)S(1)}, bf16[1,128,1,128]{1,3,2,0:T(8,128)(2,1)S(1)}, u32[]{:S(2)}, u32[]{:S(2)}) collective-permute-start(bf16[1,128,1,128]{1,3,2,0:T(8,128)(2,1)S(1)} %get-tuple-element.160), channel_id=1, source_target_pairs={{0,1},{1,2},{2,3},{4,5},{5,6},{6,7},{8,9},{9,10},{10,11},{12,13},{... | collective-permute-start | bytes 98312 | tf_op jit(solution)/shard_map/ppermute | solution.py:19
  92.5 1.3 collective-permute-start.13
  95.2 1.2 collective-permute-done.13
  99.2 0.8 multiply_reduce_fusion.5
  100.4 4.7 %collective-permute-start.18 = (bf16[1,128,1,128]{1,3,2,0:T(8,128)(2,1)S(1)}, bf16[1,128,1,128]{1,3,2,0:T(8,128)(2,1)S(1)}, u32[]{:S(2)}, u32[]{:S(2)}) collective-permute-start(bf16[1,128,1,128]{1,3,2,0:T(8,128)(2,1)S(1)} %get-tuple-element.156), channel_id=1, source_target_pairs={{0,1},{1,2},{2,3},{4,5},{5,6},{6,7},{8,9},{9,10},{10,11},{12,13},{... | collective-permute-start | bytes 98312 | tf_op jit(solution)/shard_map/ppermute | solution.py:19
  105.1 1.3 collective-permute-start.19
  106.4 1.8 collective-permute-done.19
  110.4 4.1 %collective-permute-start.20 = (bf16[1,128,1,128]{1,3,2,0:T(8,128)(2,1)S(1)}, bf16[1,128,1,128]{1,3,2,0:T(8,128)(2,1)S(1)}, u32[]{:S(2)}, u32[]{:S(2)}) collective-permute-start(bf16[1,128,1,128]{1,3,2,0:T(8,128)(2,1)S(1)} %get-tuple-element.152), channel_id=1, source_target_pairs={{0,1},{1,2},{2,3},{4,5},{5,6},{6,7},{8,9},{9,10},{10,11},{12,13},{... | collective-permute-start | bytes 98312 | tf_op jit(solution)/shard_map/ppermute | solution.py:19
  114.5 1.5 collective-permute-start.21
  116.1 1.7 multiply_reduce_fusion
  117.8 1.0 copy.381
  118.7 1.0 copy.380
  119.9 0.7 copy-done.11
  122.8 1.1 copy.260
  124.0 2.0 fusion.35
  126.0 0.7 fusion.412
  126.7 3.6 %collective-permute-start.22 = (bf16[1,64,1,256]{3,2,1,0:T(2,128)(2,1)}, bf16[1,64,1,256]{3,2,1,0:T(2,128)(2,1)}, u32[]{:S(2)}, u32[]{:S(2)}) collective-permute-start(bf16[1,64,1,256]{3,2,1,0:T(2,128)(2,1)} %get-tuple-element.104), channel_id=1, source_target_pairs={{0,1},{1,2},{2,3},{4,5},{5,6},{6,7},{8,9},{9,10},{10,11},{12,13},{... | collective-permute-start | bytes 98312 | tf_op jit(solution)/shard_map/ppermute | solution.py:19
  130.4 1.3 collective-permute-start.23
  131.7 0.7 reverse_bitcast_fusion.1
  132.4 1.0 copy.262
  133.4 1.1 copy.270
  134.5 0.8 copy.261
  136.3 0.8 copy-done.12
  138.9 0.6 convolution_add_fusion.27
  141.2 3.3 %collective-permute-start.24 = (bf16[1,64,1,256]{3,2,1,0:T(2,128)(2,1)S(1)}, bf16[1,64,1,256]{3,2,1,0:T(2,128)(2,1)S(1)}, u32[]{:S(2)}, u32[]{:S(2)}) collective-permute-start(bf16[1,64,1,256]{3,2,1,0:T(2,128)(2,1)S(1)} %get-tuple-element.100), channel_id=1, source_target_pairs={{0,1},{1,2},{2,3},{4,5},{5,6},{6,7},{8,9},{9,10},{10,11},{12,13},{... | collective-permute-start | bytes 98312 | tf_op jit(solution)/shard_map/ppermute | solution.py:19
  144.5 1.3 collective-permute-start.25
  146.0 2.8 %collective-permute-done.25 = bf16[1,64,1,256]{3,2,1,0:T(2,128)(2,1)S(1)} collective-permute-done((bf16[1,64,1,256]{3,2,1,0:T(2,128)(2,1)S(1)}, bf16[1,64,1,256]{3,2,1,0:T(2,128)(2,1)S(1)}, u32[]{:S(2)}, u32[]{:S(2)}) %collective-permute-start.25) | collective-permute-done | bytes 32800 | tf_op jit(solution)/shard_map/ppermute | solution.py:20
  151.5 4.8 %collective-permute-start.26 = (bf16[1,3,1,256]{3,1,2,0:T(4,128)(2,1)S(1)}, bf16[1,3,1,256]{3,1,2,0:T(4,128)(2,1)S(1)}, u32[]{:S(2)}, u32[]{:S(2)}) collective-permute-start(bf16[1,3,1,256]{3,1,2,0:T(4,128)(2,1)S(1)} %get-tuple-element.194), channel_id=1, source_target_pairs={{0,1},{1,2},{2,3},{4,5},{5,6},{6,7},{8,9},{9,10},{10,11},{12,13},{... | collective-permute-start | bytes 4616 | tf_op jit(solution)/shard_map/ppermute | solution.py:19
  156.4 1.6 collective-permute-start.27
  162.9 1.2 copy.303
  166.7 41.5 %all-reduce.17 = (f32[]{:T(128)}, f32[3,128,3,3]{1,3,2,0:T(4,128)}, f32[3]{0:T(128)}) all-reduce(f32[]{:T(128)S(6)} %add.1136, f32[3,128,3,3]{1,3,2,0:T(4,128)S(1)} %bitcast.1222, f32[3]{0:T(128)S(1)} %get-tuple-element.57), channel_id=1, replica_groups=mesh['clip'=8,'row'=4] {'clip','row'}, use_global_device_ids=true, to_apply=%region_8.9 | all-reduce | flops 3460 | bytes 27680 | tf_op jit(solution)/shard_map/psum | solution.py:211
  (378 shorter events, 44.3 us)
Async XLA Ops:
  0.6 7.0 %copy-start.17 = (bf16[3,128,3,3]{1,3,2,0:T(4,128)(2,1)S(1)}, bf16[3,128,3,3]{1,3,2,0:T(4,128)(2,1)}, u32[]{:S(2)}) copy-start(bf16[3,128,3,3]{1,3,2,0:T(4,128)(2,1)} %param.24) | copy-start | bytes 20740
  0.6 7.1 %copy-start = (bf16[1,128,8,256]{3,2,1,0:T(8,128)(2,1)S(1)}, bf16[1,128,8,256]{3,2,1,0:T(8,128)(2,1)}, u32[]{:S(2)}) copy-start(bf16[1,128,8,256]{3,2,1,0:T(8,128)(2,1)} %param.23) | copy-start | bytes 1572868
  3.4 12.2 %collective-permute-start = (f32[1,3,256]{2,1,0:T(4,128)S(1)}, f32[1,3,256]{2,1,0:T(4,128)S(1)}, u32[]{:S(2)}, u32[]{:S(2)}) collective-permute-start(f32[1,3,256]{2,1,0:T(4,128)S(1)} %fusion.18), channel_id=1, source_target_pairs={{0,1},{1,2},{2,3},{4,5},{5,6},{6,7},{8,9},{9,10},{10,11},{12,13},{... | collective-permute-start | bytes 9224 | tf_op jit(solution)/shard_map/ppermute | solution.py:28
  6.4 9.2 %collective-permute-start.1 = (f32[1,3,256]{2,1,0:T(4,128)S(1)}, f32[1,3,256]{2,1,0:T(4,128)S(1)}, u32[]{:S(2)}, u32[]{:S(2)}) collective-permute-start(f32[1,3,256]{2,1,0:T(4,128)S(1)} %fusion.17), channel_id=1, source_target_pairs={{1,0},{2,1},{3,2},{5,4},{6,5},{7,6},{9,8},{10,9},{11,10},{13,12},{... | collective-permute-start | bytes 9224 | tf_op jit(solution)/shard_map/ppermute | solution.py:28
  10.6 0.7 copy-start.18
  10.6 0.7 copy-start.37
  10.6 1.2 copy-start.1
  10.7 1.9 copy-start.34
  14.0 0.9 copy-start.4
  14.2 1.4 copy-start.21
  14.2 1.4 copy-start.27
  14.2 1.5 copy-start.33
  14.2 1.5 copy-start.36
  15.8 12.1 %collective-permute-start.2 = (bf16[1,3,1,256]{3,1,2,0:T(4,128)(2,1)S(1)}, bf16[1,3,1,256]{3,1,2,0:T(4,128)(2,1)S(1)}, u32[]{:S(2)}, u32[]{:S(2)}) collective-permute-start(bf16[1,3,1,256]{3,1,2,0:T(4,128)(2,1)S(1)} %get-tuple-element.202), channel_id=1, source_target_pairs={{0,1},{1,2},{2,3},{4,5},{5,6},{6,7},{8,9},{9,10},{10,11},{12,13},{... | collective-permute-start | bytes 4616 | tf_op jit(solution)/shard_map/ppermute | solution.py:19
  20.9 6.9 %collective-permute-start.3 = (bf16[1,3,1,256]{3,1,2,0:T(4,128)(2,1)S(1)}, bf16[1,3,1,256]{3,1,2,0:T(4,128)(2,1)S(1)}, u32[]{:S(2)}, u32[]{:S(2)}) collective-permute-start(bf16[1,3,1,256]{3,1,2,0:T(4,128)(2,1)S(1)} %get-tuple-element.203), channel_id=1, source_target_pairs={{1,0},{2,1},{3,2},{5,4},{6,5},{7,6},{9,8},{10,9},{11,10},{13,12},{... | collective-permute-start | bytes 4616 | tf_op jit(solution)/shard_map/ppermute | solution.py:20
  22.2 8.5 %collective-permute-start.6 = (bf16[1,3,1,256]{3,1,2,0:T(4,128)(2,1)S(1)}, bf16[1,3,1,256]{3,1,2,0:T(4,128)(2,1)S(1)}, u32[]{:S(2)}, u32[]{:S(2)}) collective-permute-start(bf16[1,3,1,256]{3,1,2,0:T(4,128)(2,1)S(1)} %get-tuple-element.198), channel_id=1, source_target_pairs={{0,1},{1,2},{2,3},{4,5},{5,6},{6,7},{8,9},{9,10},{10,11},{12,13},{... | collective-permute-start | bytes 4616 | tf_op jit(solution)/shard_map/ppermute | solution.py:19
  26.5 4.3 %collective-permute-start.7 = (bf16[1,3,1,256]{3,1,2,0:T(4,128)(2,1)S(1)}, bf16[1,3,1,256]{3,1,2,0:T(4,128)(2,1)S(1)}, u32[]{:S(2)}, u32[]{:S(2)}) collective-permute-start(bf16[1,3,1,256]{3,1,2,0:T(4,128)(2,1)S(1)} %get-tuple-element.199), channel_id=1, source_target_pairs={{1,0},{2,1},{3,2},{5,4},{6,5},{7,6},{9,8},{10,9},{11,10},{13,12},{... | collective-permute-start | bytes 4616 | tf_op jit(solution)/shard_map/ppermute | solution.py:20
  33.2 0.7 copy-start.22
  34.3 11.5 %collective-permute-start.8 = (bf16[1,64,1,256]{3,2,1,0:T(2,128)(2,1)S(1)}, bf16[1,64,1,256]{3,2,1,0:T(2,128)(2,1)S(1)}, u32[]{:S(2)}, u32[]{:S(2)}) collective-permute-start(bf16[1,64,1,256]{3,2,1,0:T(2,128)(2,1)S(1)} %get-tuple-element.108), channel_id=1, source_target_pairs={{0,1},{1,2},{2,3},{4,5},{5,6},{6,7},{8,9},{9,10},{10,11},{12,13},{... | collective-permute-start | bytes 98312 | tf_op jit(solution)/shard_map/ppermute | solution.py:19
  38.5 7.2 %collective-permute-start.9 = (bf16[1,64,1,256]{3,2,1,0:T(2,128)(2,1)S(1)}, bf16[1,64,1,256]{3,2,1,0:T(2,128)(2,1)S(1)}, u32[]{:S(2)}, u32[]{:S(2)}) collective-permute-start(bf16[1,64,1,256]{3,2,1,0:T(2,128)(2,1)S(1)} %get-tuple-element.109), channel_id=1, source_target_pairs={{1,0},{2,1},{3,2},{5,4},{6,5},{7,6},{9,8},{10,9},{11,10},{13,12},{... | collective-permute-start | bytes 98312 | tf_op jit(solution)/shard_map/ppermute | solution.py:20
  40.1 6.1 %collective-permute-start.4 = (bf16[1,64,1,256]{3,2,1,0:T(2,128)(2,1)S(1)}, bf16[1,64,1,256]{3,2,1,0:T(2,128)(2,1)S(1)}, u32[]{:S(2)}, u32[]{:S(2)}) collective-permute-start(bf16[1,64,1,256]{3,2,1,0:T(2,128)(2,1)S(1)} %get-tuple-element.112), channel_id=1, source_target_pairs={{0,1},{1,2},{2,3},{4,5},{5,6},{6,7},{8,9},{9,10},{10,11},{12,13},{... | collective-permute-start | bytes 98312 | tf_op jit(solution)/shard_map/ppermute | solution.py:19
  44.3 4.4 %collective-permute-start.5 = (bf16[1,64,1,256]{3,2,1,0:T(2,128)(2,1)S(1)}, bf16[1,64,1,256]{3,2,1,0:T(2,128)(2,1)S(1)}, u32[]{:S(2)}, u32[]{:S(2)}) collective-permute-start(bf16[1,64,1,256]{3,2,1,0:T(2,128)(2,1)S(1)} %get-tuple-element.113), channel_id=1, source_target_pairs={{1,0},{2,1},{3,2},{5,4},{6,5},{7,6},{9,8},{10,9},{11,10},{13,12},{... | collective-permute-start | bytes 98312 | tf_op jit(solution)/shard_map/ppermute | solution.py:20
  49.4 0.9 copy-start.6
  64.5 1.8 copy-start.14
  66.5 10.7 %collective-permute-start.14 = (bf16[1,64,1,128]{1,3,2,0:T(8,128)(2,1)S(1)}, bf16[1,64,1,128]{1,3,2,0:T(8,128)(2,1)S(1)}, u32[]{:S(2)}, u32[]{:S(2)}) collective-permute-start(bf16[1,64,1,128]{1,3,2,0:T(8,128)(2,1)S(1)} %get-tuple-element.172), channel_id=1, source_target_pairs={{0,1},{1,2},{2,3},{4,5},{5,6},{6,7},{8,9},{9,10},{10,11},{12,13},{... | collective-permute-start | bytes 49160 | tf_op jit(solution)/shard_map/ppermute | solution.py:19
  71.4 6.0 %copy-start.5 = (bf16[128,64,3,3]{0,1,3,2:T(8,128)(2,1)S(1)}, bf16[128,64,3,3]{0,1,3,2:T(8,128)(2,1)}, u32[]{:S(2)}) copy-start(bf16[128,64,3,3]{0,1,3,2:T(8,128)(2,1)} %param.31) | copy-start | bytes 442372
  71.4 5.8 %collective-permute-start.15 = (bf16[1,64,1,128]{1,3,2,0:T(8,128)(2,1)S(1)}, bf16[1,64,1,128]{1,3,2,0:T(8,128)(2,1)S(1)}, u32[]{:S(2)}, u32[]{:S(2)}) collective-permute-start(bf16[1,64,1,128]{1,3,2,0:T(8,128)(2,1)S(1)} %get-tuple-element.173), channel_id=1, source_target_pairs={{1,0},{2,1},{3,2},{5,4},{6,5},{7,6},{9,8},{10,9},{11,10},{13,12},{... | collective-permute-start | bytes 49160 | tf_op jit(solution)/shard_map/ppermute | solution.py:20
  72.8 4.9 %collective-permute-start.10 = (bf16[1,64,1,128]{1,3,2,0:T(8,128)(2,1)S(1)}, bf16[1,64,1,128]{1,3,2,0:T(8,128)(2,1)S(1)}, u32[]{:S(2)}, u32[]{:S(2)}) collective-permute-start(bf16[1,64,1,128]{1,3,2,0:T(8,128)(2,1)S(1)} %get-tuple-element.164), channel_id=1, source_target_pairs={{0,1},{1,2},{2,3},{4,5},{5,6},{6,7},{8,9},{9,10},{10,11},{12,13},{... | collective-permute-start | bytes 49160 | tf_op jit(solution)/shard_map/ppermute | solution.py:19
  75.9 3.9 %collective-permute-start.11 = (bf16[1,64,1,128]{1,3,2,0:T(8,128)(2,1)S(1)}, bf16[1,64,1,128]{1,3,2,0:T(8,128)(2,1)S(1)}, u32[]{:S(2)}, u32[]{:S(2)}) collective-permute-start(bf16[1,64,1,128]{1,3,2,0:T(8,128)(2,1)S(1)} %get-tuple-element.165), channel_id=1, source_target_pairs={{1,0},{2,1},{3,2},{5,4},{6,5},{7,6},{9,8},{10,9},{11,10},{13,12},{... | collective-permute-start | bytes 49160 | tf_op jit(solution)/shard_map/ppermute | solution.py:20
  80.3 0.9 copy-start.16
  83.6 10.2 %collective-permute-start.16 = (bf16[1,128,1,128]{1,3,2,0:T(8,128)(2,1)S(1)}, bf16[1,128,1,128]{1,3,2,0:T(8,128)(2,1)S(1)}, u32[]{:S(2)}, u32[]{:S(2)}) collective-permute-start(bf16[1,128,1,128]{1,3,2,0:T(8,128)(2,1)S(1)} %get-tuple-element.168), channel_id=1, source_target_pairs={{0,1},{1,2},{2,3},{4,5},{5,6},{6,7},{8,9},{9,10},{10,11},{12,13},{... | collective-permute-start | bytes 98312 | tf_op jit(solution)/shard_map/ppermute | solution.py:19
  88.1 5.7 %collective-permute-start.17 = (bf16[1,128,1,128]{1,3,2,0:T(8,128)(2,1)S(1)}, bf16[1,128,1,128]{1,3,2,0:T(8,128)(2,1)S(1)}, u32[]{:S(2)}, u32[]{:S(2)}) collective-permute-start(bf16[1,128,1,128]{1,3,2,0:T(8,128)(2,1)S(1)} %get-tuple-element.169), channel_id=1, source_target_pairs={{1,0},{2,1},{3,2},{5,4},{6,5},{7,6},{9,8},{10,9},{11,10},{13,12},{... | collective-permute-start | bytes 98312 | tf_op jit(solution)/shard_map/ppermute | solution.py:20
  89.5 5.7 %collective-permute-start.12 = (bf16[1,128,1,128]{1,3,2,0:T(8,128)(2,1)S(1)}, bf16[1,128,1,128]{1,3,2,0:T(8,128)(2,1)S(1)}, u32[]{:S(2)}, u32[]{:S(2)}) collective-permute-start(bf16[1,128,1,128]{1,3,2,0:T(8,128)(2,1)S(1)} %get-tuple-element.160), channel_id=1, source_target_pairs={{0,1},{1,2},{2,3},{4,5},{5,6},{6,7},{8,9},{9,10},{10,11},{12,13},{... | collective-permute-start | bytes 98312 | tf_op jit(solution)/shard_map/ppermute | solution.py:19
  92.5 3.9 %collective-permute-start.13 = (bf16[1,128,1,128]{1,3,2,0:T(8,128)(2,1)S(1)}, bf16[1,128,1,128]{1,3,2,0:T(8,128)(2,1)S(1)}, u32[]{:S(2)}, u32[]{:S(2)}) collective-permute-start(bf16[1,128,1,128]{1,3,2,0:T(8,128)(2,1)S(1)} %get-tuple-element.161), channel_id=1, source_target_pairs={{1,0},{2,1},{3,2},{5,4},{6,5},{7,6},{9,8},{10,9},{11,10},{13,12},{... | collective-permute-start | bytes 98312 | tf_op jit(solution)/shard_map/ppermute | solution.py:20
  98.5 0.7 copy-start.32
  98.5 0.7 copy-start.38
  100.3 8.0 %copy-start.8 = (bf16[128,128,3,3]{0,1,3,2:T(8,128)(2,1)S(1)}, bf16[128,128,3,3]{0,1,3,2:T(8,128)(2,1)}, u32[]{:S(2)}) copy-start(bf16[128,128,3,3]{0,1,3,2:T(8,128)(2,1)} %reverse_bitcast_fusion) | copy-start | bytes 884740
  100.4 6.0 %collective-permute-start.18 = (bf16[1,128,1,128]{1,3,2,0:T(8,128)(2,1)S(1)}, bf16[1,128,1,128]{1,3,2,0:T(8,128)(2,1)S(1)}, u32[]{:S(2)}, u32[]{:S(2)}) collective-permute-start(bf16[1,128,1,128]{1,3,2,0:T(8,128)(2,1)S(1)} %get-tuple-element.156), channel_id=1, source_target_pairs={{0,1},{1,2},{2,3},{4,5},{5,6},{6,7},{8,9},{9,10},{10,11},{12,13},{... | collective-permute-start | bytes 98312 | tf_op jit(solution)/shard_map/ppermute | solution.py:19
  105.1 3.1 %collective-permute-start.19 = (bf16[1,128,1,128]{1,3,2,0:T(8,128)(2,1)S(1)}, bf16[1,128,1,128]{1,3,2,0:T(8,128)(2,1)S(1)}, u32[]{:S(2)}, u32[]{:S(2)}) collective-permute-start(bf16[1,128,1,128]{1,3,2,0:T(8,128)(2,1)S(1)} %get-tuple-element.157), channel_id=1, source_target_pairs={{1,0},{2,1},{3,2},{5,4},{6,5},{7,6},{9,8},{10,9},{11,10},{13,12},{... | collective-permute-start | bytes 98312 | tf_op jit(solution)/shard_map/ppermute | solution.py:20
  109.9 6.2 %copy-start.2 = (f32[64,2048]{1,0:T(8,128)S(1)}, f32[64,2048]{1,0:T(8,128)}, u32[]{:S(2)}) copy-start(f32[64,2048]{1,0:T(8,128)} %get-tuple-element.63) | copy-start | bytes 1572868
  109.9 6.2 %copy-start.25 = (f32[64]{0:T(128)S(1)}, f32[64]{0:T(128)}, u32[]{:S(2)}) copy-start(f32[64]{0:T(128)} %param.30) | copy-start | bytes 772
  109.9 6.1 %copy-start.30 = (f32[64]{0:T(128)S(1)}, f32[64]{0:T(128)}, u32[]{:S(2)}) copy-start(f32[64]{0:T(128)} %broadcast_multiply_fusion.1) | copy-start | bytes 772
  109.9 6.1 %copy-start.35 = (f32[64]{0:T(128)S(1)}, f32[64]{0:T(128)}, u32[]{:S(2)}) copy-start(f32[64]{0:T(128)} %param.35) | copy-start | bytes 772
  110.3 7.5 %copy-start.9 = (f32[512,128]{1,0:T(8,128)}, f32[512,128]{1,0:T(8,128)S(1)}, u32[]{:S(2)}) copy-start(f32[512,128]{1,0:T(8,128)S(1)} %fusion.9) | copy-start | bytes 786436
  110.4 9.3 %collective-permute-start.20 = (bf16[1,128,1,128]{1,3,2,0:T(8,128)(2,1)S(1)}, bf16[1,128,1,128]{1,3,2,0:T(8,128)(2,1)S(1)}, u32[]{:S(2)}, u32[]{:S(2)}) collective-permute-start(bf16[1,128,1,128]{1,3,2,0:T(8,128)(2,1)S(1)} %get-tuple-element.152), channel_id=1, source_target_pairs={{0,1},{1,2},{2,3},{4,5},{5,6},{6,7},{8,9},{9,10},{10,11},{12,13},{... | collective-permute-start | bytes 98312 | tf_op jit(solution)/shard_map/ppermute | solution.py:19
  114.5 5.2 %collective-permute-start.21 = (bf16[1,128,1,128]{1,3,2,0:T(8,128)(2,1)S(1)}, bf16[1,128,1,128]{1,3,2,0:T(8,128)(2,1)S(1)}, u32[]{:S(2)}, u32[]{:S(2)}) collective-permute-start(bf16[1,128,1,128]{1,3,2,0:T(8,128)(2,1)S(1)} %get-tuple-element.153), channel_id=1, source_target_pairs={{1,0},{2,1},{3,2},{5,4},{6,5},{7,6},{9,8},{10,9},{11,10},{13,12},{... | collective-permute-start | bytes 98312 | tf_op jit(solution)/shard_map/ppermute | solution.py:20
  117.7 1.9 copy-start.19
  119.7 0.9 copy-start.11
  119.9 1.4 copy-start.10
  124.0 7.7 %copy-start.7 = (bf16[64,64,3,3]{1,0,3,2:T(8,128)(2,1)S(1)}, bf16[64,64,3,3]{1,0,3,2:T(8,128)(2,1)}, u32[]{:S(2)}) copy-start(bf16[64,64,3,3]{1,0,3,2:T(8,128)(2,1)} %param.29) | copy-start | bytes 221188
  126.0 6.4 %copy-start.3 = (bf16[1,64,8,256]{3,2,1,0:T(8,128)(2,1)}, bf16[1,64,8,256]{3,2,1,0:T(8,128)(2,1)S(1)}, u32[]{:S(2)}) copy-start(bf16[1,64,8,256]{3,2,1,0:T(8,128)(2,1)S(1)} %fusion.35) | copy-start | bytes 786436
  126.7 7.8 %collective-permute-start.22 = (bf16[1,64,1,256]{3,2,1,0:T(2,128)(2,1)}, bf16[1,64,1,256]{3,2,1,0:T(2,128)(2,1)}, u32[]{:S(2)}, u32[]{:S(2)}) collective-permute-start(bf16[1,64,1,256]{3,2,1,0:T(2,128)(2,1)} %get-tuple-element.104), channel_id=1, source_target_pairs={{0,1},{1,2},{2,3},{4,5},{5,6},{6,7},{8,9},{9,10},{10,11},{12,13},{... | collective-permute-start | bytes 98312 | tf_op jit(solution)/shard_map/ppermute | solution.py:19
  130.4 5.0 %collective-permute-start.23 = (bf16[1,64,1,256]{3,2,1,0:T(2,128)(2,1)}, bf16[1,64,1,256]{3,2,1,0:T(2,128)(2,1)S(1)}, u32[]{:S(2)}, u32[]{:S(2)}) collective-permute-start(bf16[1,64,1,256]{3,2,1,0:T(2,128)(2,1)} %get-tuple-element.105), channel_id=1, source_target_pairs={{1,0},{2,1},{3,2},{5,4},{6,5},{7,6},{9,8},{10,9},{11,10},{13,12},{... | collective-permute-start | bytes 98312 | tf_op jit(solution)/shard_map/ppermute | solution.py:20
  136.2 0.9 copy-start.12
  137.6 1.0 copy-start.13
  137.7 1.2 copy-start.15
  137.7 1.2 copy-start.20
  137.7 1.2 copy-start.26
  137.7 1.2 copy-start.31
  141.2 4.8 %collective-permute-start.24 = (bf16[1,64,1,256]{3,2,1,0:T(2,128)(2,1)S(1)}, bf16[1,64,1,256]{3,2,1,0:T(2,128)(2,1)S(1)}, u32[]{:S(2)}, u32[]{:S(2)}) collective-permute-start(bf16[1,64,1,256]{3,2,1,0:T(2,128)(2,1)S(1)} %get-tuple-element.100), channel_id=1, source_target_pairs={{0,1},{1,2},{2,3},{4,5},{5,6},{6,7},{8,9},{9,10},{10,11},{12,13},{... | collective-permute-start | bytes 98312 | tf_op jit(solution)/shard_map/ppermute | solution.py:19
  144.5 4.2 %collective-permute-start.25 = (bf16[1,64,1,256]{3,2,1,0:T(2,128)(2,1)S(1)}, bf16[1,64,1,256]{3,2,1,0:T(2,128)(2,1)S(1)}, u32[]{:S(2)}, u32[]{:S(2)}) collective-permute-start(bf16[1,64,1,256]{3,2,1,0:T(2,128)(2,1)S(1)} %get-tuple-element.101), channel_id=1, source_target_pairs={{1,0},{2,1},{3,2},{5,4},{6,5},{7,6},{9,8},{10,9},{11,10},{13,12},{... | collective-permute-start | bytes 98312 | tf_op jit(solution)/shard_map/ppermute | solution.py:20
  150.3 0.9 copy-start.28
  151.5 7.7 %collective-permute-start.26 = (bf16[1,3,1,256]{3,1,2,0:T(4,128)(2,1)S(1)}, bf16[1,3,1,256]{3,1,2,0:T(4,128)(2,1)S(1)}, u32[]{:S(2)}, u32[]{:S(2)}) collective-permute-start(bf16[1,3,1,256]{3,1,2,0:T(4,128)(2,1)S(1)} %get-tuple-element.194), channel_id=1, source_target_pairs={{0,1},{1,2},{2,3},{4,5},{5,6},{6,7},{8,9},{9,10},{10,11},{12,13},{... | collective-permute-start | bytes 4616 | tf_op jit(solution)/shard_map/ppermute | solution.py:19
  156.4 3.1 %collective-permute-start.27 = (bf16[1,3,1,256]{3,1,2,0:T(4,128)(2,1)S(1)}, bf16[1,3,1,256]{3,1,2,0:T(4,128)(2,1)S(1)}, u32[]{:S(2)}, u32[]{:S(2)}) collective-permute-start(bf16[1,3,1,256]{3,1,2,0:T(4,128)(2,1)S(1)} %get-tuple-element.195), channel_id=1, source_target_pairs={{1,0},{2,1},{3,2},{5,4},{6,5},{7,6},{9,8},{10,9},{11,10},{13,12},{... | collective-permute-start | bytes 4616 | tf_op jit(solution)/shard_map/ppermute | solution.py:20
  (3 other events, 2.0 us)
where the time goes:
time: 210 us; the launch traced here: 208 us
  starting transfers between devices  75.1 us (36%)
  blocking collectives  41.5 us (20%)
  matrix products  32.7 us (16%)
  local copies, waits for them, and re-layouts  32.1 us (15%)
  other arithmetic  11.8 us (6%)
  waiting for transfers between devices  10.5 us (5%)
  between operations  4.34 us (2%)
    ppermute x13, starting transfers between devices, padded_2(): before = lax.ppermute(last, axis, up)  53.9 us
    psum x1, blocking collectives, local(): lax.psum((part_one + part_two, weight_grad, bias_grad), ('clip', 'row'))  41.5 us
    dot_general x126, matrix products, conv_valid(): jnp.dot(weight[:, :, row_shift, col_shift], piece.reshape(channels, row_c...  29.1 us
    ppermute x13, starting transfers between devices, padded_2(): after = lax.ppermute(leading, axis, down)  17.6 us
    unnamed x129, local copies, waits for them, and re-layouts  11.2 us
    ppermute x13, waiting for transfers between devices, padded_2(): after = lax.ppermute(leading, axis, down)  10.5 us
  transfers between devices with their start and end apart: 28, of which 7 were waited for; matrix products, arithmetic and copies ran while one was open for 10% of the time, Pallas kernels for 0%

commit v1 on v0

v1 whole, which is shorter than its diff:
```python
import functools
import math

import jax
import jax.numpy as jnp
from jax import lax
from jax.experimental import pallas as pl
from jax.experimental.pallas import tpu as pltpu
from jax.sharding import PartitionSpec as P

shift_values = [-0.03, -0.088, -0.188]
scale_values = [0.458, 0.448, 0.45]

F32, BF16 = jnp.float32, jnp.bfloat16


def colshift(v, b, width):
    if b == 1:
        return v
    lanes = v.shape[1]
    col = lax.broadcasted_iota(jnp.int32, v.shape, 1) % width
    if b == 0:
        return jnp.where(col == 0, 0.0, pltpu.roll(v, 1, 1))
    return jnp.where(col == width - 1, 0.0, pltpu.roll(v, lanes - 1, 1))


def rounded(v):
    return v.astype(BF16).astype(F32)


def dot(a, b):
    return jnp.dot(a, b, preferred_element_type=F32)


def dot_split(v, m):
    high = v.astype(BF16)
    low = (v - high.astype(F32)).astype(BF16)
    return dot(high, m) + dot(low, m)


def cdf_of(v):
    return 0.5 + 0.5 * lax.erf(v * (1.0 / math.sqrt(2.0)))


def gelu_slope(v, cdf):
    return cdf + v * (jnp.exp(-0.5 * v * v) * (1.0 / math.sqrt(2.0 * math.pi)))


def unit_of(f):
    inv = lax.rsqrt(jnp.sum(f * f, 0, keepdims=True) + 1e-06)
    return f * inv, inv


def lpips(f_dec, f_tgt, lin, count):
    unit, inv = unit_of(f_dec)
    unit_tgt, _ = unit_of(f_tgt)
    differ = unit - unit_tgt
    scaled = lin * differ * (1.0 / count)
    part = jnp.sum(scaled * differ, 0, keepdims=True)
    grad = 2.0 * scaled
    return part, (grad - unit * jnp.sum(grad * unit, 0, keepdims=True)) * inv


NAMES = (
    "img_t", "img_d", "pb", "xt", "xd", "x3t", "x3d", "x4t", "x4d", "xg4", "xg3", "xg2", "act2t",
    "act4t", "gf1", "s1", "s2", "s3", "gdec", "lacc", "slot_r", "slot_c", "w2", "w2t", "w3",
    "w3t", "w4", "w4t", "few", "vec", "tbuf", "wg",
)
MESSAGES = ("t", "d", "pt", "pd", "3t", "3d", "g4", "g3", "g2", "gd")


def message_shapes(C1, C2, W):
    Wh = W // 2
    return {
        "t": ((8, 2 * W), F32),
        "d": ((8, 3 * W), F32),
        "pt": ((C1, Wh), BF16),
        "pd": ((C1, Wh), BF16),
        "3t": ((C2, Wh), BF16),
        "3d": ((C2, Wh), BF16),
        "g4": ((C2, Wh), BF16),
        "g3": ((C2, Wh), BF16),
        "g2": ((C1, W), BF16),
        "gd": ((8, 2 * W), F32),
    }


def kernel_body(
    dims, feat, tgt, wo_raw, w1_raw, w2_raw, w3_raw, w4_raw, ob_raw, b1_raw, b2_raw, l1_raw,
    b3_raw, b4_raw, l2_raw, fg_out, red_out, *scratch
):
    R, W, C1, C2, CF, nrow, nclip = dims
    Wh, Rh = W // 2, R // 2
    H = R * nrow
    s = dict(zip(NAMES, scratch))
    rest = scratch[len(NAMES):]
    w2, w2t, w3, w3t, w4, w4t = (s[n] for n in ("w2", "w2t", "w3", "w3t", "w4", "w4t"))
    bufs = {}
    for k, name in enumerate(MESSAGES):
        bufs[name] = rest[4 * k : 4 * k + 4]
    send_sem, recv_sem, all_send, all_recv = rest[4 * len(MESSAGES):]

    me_r, me_c = lax.axis_index("row"), lax.axis_index("clip")
    keep_up = jnp.where(me_r > 0, 1.0, 0.0).astype(F32)
    keep_dn = jnp.where(me_r < nrow - 1, 1.0, 0.0).astype(F32)
    up, dn = (me_r + nrow - 1) % nrow, (me_r + 1) % nrow

    barrier = pltpu.get_barrier_semaphore()
    for k in range(1, nrow):
        pl.semaphore_signal(
            barrier, inc=1, device_id={"row": (me_r + k) % nrow}, device_id_type=pl.DeviceIdType.MESH
        )
    for k in range(1, nclip):
        pl.semaphore_signal(
            barrier, inc=1, device_id={"clip": (me_c + k) % nclip}, device_id_type=pl.DeviceIdType.MESH
        )

    def copies(name):
        k = MESSAGES.index(name)
        su, sd, ru, rd = bufs[name]
        to_up = pltpu.make_async_remote_copy(
            src_ref=su, dst_ref=rd, send_sem=send_sem.at[2 * k], recv_sem=recv_sem.at[2 * k],
            device_id={"row": up}, device_id_type=pl.DeviceIdType.MESH,
        )
        to_dn = pltpu.make_async_remote_copy(
            src_ref=sd, dst_ref=ru, send_sem=send_sem.at[2 * k + 1], recv_sem=recv_sem.at[2 * k + 1],
            device_id={"row": dn}, device_id_type=pl.DeviceIdType.MESH,
        )
        return to_up, to_dn

    def send(name, up_value, dn_value):
        su, sd, _, _ = bufs[name]
        su[...] = up_value.astype(su.dtype)
        sd[...] = dn_value.astype(sd.dtype)
        a, b = copies(name)
        a.start()
        b.start()

    def receive(name):
        a, b = copies(name)
        a.wait()
        b.wait()
        _, _, ru, rd = bufs[name]
        return ru[...].astype(F32) * keep_up, rd[...].astype(F32) * keep_dn

    def span(row, count, width=W):
        start = row * width
        if not isinstance(start, int):
            start = pl.multiple_of(start, width)
        return pl.ds(start, count * width)

    def store3(ref, row, value, width):
        C = value.shape[0]
        for b in range(3):
            ref[b * C : (b + 1) * C, span(row, value.shape[1] // width, width)] = colshift(
                value, b, width
            ).astype(BF16)

    def store24(ref, row, value):
        ref[:, span(row, value.shape[1] // W)] = jnp.concatenate(
            [colshift(value, b, W) for b in range(3)], 0
        )

    def im72(ref, row, count):
        return jnp.concatenate([ref[:, span(row + a, count)] for a in range(3)], 0).astype(BF16)

    def conv(weight, ref, row, count, width):
        total = dot(weight[0], ref[:, span(row, count, width)])
        for a in range(1, 3):
            total = total + dot(weight[a], ref[:, span(row + a, count, width)])
        return total

    vec = s["vec"]
    vec[...] = jnp.zeros_like(vec)
    for k, ref in enumerate((b1_raw, b2_raw, l1_raw, b3_raw, b4_raw, l2_raw)):
        vec[k : k + 1, : ref.shape[1]] = ref[...]
    columns = vec[...].T
    b1, b2, lin1 = (columns[:C1, k : k + 1] for k in range(3))
    b3, b4, lin2 = (columns[:C2, k : k + 1] for k in range(3, 6))
    sub = lax.broadcasted_iota(jnp.int32, (8, 1), 0)

    def column(values, fill):
        out = jnp.full((8, 1), fill, F32)
        for k in range(3):
            out = jnp.where(sub == k, values[k], out)
        return out

    obias = column([ob_raw[k] for k in range(3)], 0.0)
    shift, scale = column(shift_values, 0.0), column(scale_values, 1.0)
    lane = lambda shape, dim: lax.broadcasted_iota(jnp.int32, shape, dim)
    pool_m = jnp.where(lane((W, Wh), 0) // 2 == lane((W, Wh), 1), 0.25, 0.0).astype(BF16)
    up_m = jnp.where(lane((Wh, W), 1) // 2 == lane((Wh, W), 0), 0.25, 0.0).astype(BF16)

    few = s["few"]
    few[...] = jnp.zeros_like(few)

    def spread(k, raw, flip):
        for i in range(3):
            for a in range(3):
                rows = raw[i, 2 - a if flip else a].astype(F32)
                for b in range(3):
                    c = 2 - b if flip else b
                    at = (a * 3 + b) * 8 + i
                    few[k, at : at + 1, : rows.shape[1]] = rows[c : c + 1]

    def normal(v):
        return rounded((v - shift) / scale)

    pb = s["pb"]

    def partials(weight, source, rows):
        for i in rows:
            T = dot(weight, source(i))
            for a in range(3):
                part = colshift(T[24 * a : 24 * a + 8], 0, W)
                part = part + T[24 * a + 8 : 24 * a + 16]
                part = part + colshift(T[24 * a + 16 : 24 * a + 24], 2, W)
                at = span(i + 2 - a, 1)
                pb[:, at] = pb[:, at] + part

    spread(0, wo_raw, False)
    spread(1, w1_raw, False)
    w1 = few[1].T[:C1, :72].astype(BF16)
    tbuf = s["tbuf"]
    tbuf[...] = jnp.zeros_like(tbuf)
    for i in range(3):
        rows = tgt[i].astype(F32)
        for r in range(R):
            tbuf[i : i + 1, r * W : (r + 1) * W] = rows[r : r + 1]
    t_img = normal(tbuf[...])
    pl.semaphore_wait(barrier, nrow - 1 + nclip - 1)
    send("t", t_img[:, : 2 * W], t_img[:, (R - 2) * W :])
    store24(s["img_t"], 2, t_img)
    pb[...] = jnp.zeros_like(pb)
    partials(few[0, :72, :CF].astype(BF16), lambda i: feat[:, span(i, 1)], range(R))
    send("d", pb[:, : 3 * W], pb[:, (R - 1) * W :])

    for a in range(3):
        for b in range(3):
            w2[a, :, b * C1 : (b + 1) * C1] = w2_raw[a, b]
            w3[a, :, b * C1 : (b + 1) * C1] = w3_raw[a, b].T
            w3t[a, :, b * C2 : (b + 1) * C2] = w3_raw[2 - a, 2 - b]
            w4[a, :, b * C2 : (b + 1) * C2] = w4_raw[a, b]

    above, below = receive("t")
    store24(s["img_t"], 0, above)
    store24(s["img_t"], R + 2, below)

    def block_one(img, x, tail, save):
        def first(i, carry):
            row = 2 * i
            pre = dot(w1, im72(img, row, 2)) + b1
            cdf = cdf_of(pre)
            act = pre * cdf
            if save:
                s["s1"][:, span(row, 2)] = gelu_slope(pre, cdf)
            col = lax.broadcasted_iota(jnp.int32, (1, 2 * W), 1)
            m_first = jnp.where(i == 0, keep_up, 1.0)
            m_last = jnp.where(i == R // 2, keep_dn, 1.0)
            act = act * jnp.where(col < W, m_first, m_last)
            store3(x, row, act, W)
            return carry

        lax.fori_loop(0, R // 2 + 1, first, 0)

        def second(i, carry):
            pre = conv(w2, x, 2 * i, 2, W) + b2
            cdf = cdf_of(pre)
            act = pre * cdf
            tail(i, pre, cdf, act)
            return carry

        lax.fori_loop(0, Rh, second, 0)

    def pooled_of(act):
        return rounded(dot_split(act[:, :W] + act[:, W:], pool_m))

    def tail_target(i, pre, cdf, act):
        s["act2t"][:, span(2 * i, 2)] = act
        store3(s["x3t"], i + 1, pooled_of(act), Wh)

    def tail_decoded(i, pre, cdf, act):
        store3(s["x3d"], i + 1, pooled_of(act), Wh)
        s["s2"][:, span(2 * i, 2)] = gelu_slope(pre, cdf)
        part, grad = lpips(act, s["act2t"][:, span(2 * i, 2)], lin1, float(H * W))
        s["gf1"][:, span(2 * i, 2)] = grad
        s["lacc"][0:1, :] = s["lacc"][0:1, :] + part

    s["lacc"][...] = jnp.zeros_like(s["lacc"])
    block_one(s["img_t"], s["xt"], tail_target, False)

    def edges(ref, C, rows, width):
        return ref[C : 2 * C, width : 2 * width], ref[C : 2 * C, rows * width : (rows + 1) * width]

    def halo(name, ref, rows, width):
        above, below = receive(name)
        store3(ref, 0, above, width)
        store3(ref, rows + 1, below, width)

    send("pt", *edges(s["x3t"], C1, Rh, Wh))

    above, below = receive("d")
    zero = jnp.zeros((8, W), F32)
    sums = pb[...] + jnp.concatenate(
        [above[:, W:], jnp.zeros((8, (R - 2) * W), F32), below[:, : 2 * W]], 1
    )
    dec = jnp.concatenate([above[:, :W], sums, below[:, 2 * W :]], 1)
    d_img = normal(rounded(dec + obias))
    col = lax.broadcasted_iota(jnp.int32, (1, (R + 4) * W), 1)
    d_img = d_img * jnp.where(col < 2 * W, keep_up, jnp.where(col < (R + 2) * W, 1.0, keep_dn))
    store24(s["img_d"], 0, d_img)
    block_one(s["img_d"], s["xd"], tail_decoded, True)
    send("pd", *edges(s["x3d"], C1, Rh, Wh))

    def block_three(name, x3, x4, save):
        halo(name, x3, Rh, Wh)
        pre = conv(w3, x3, 0, Rh, Wh) + b3
        cdf = cdf_of(pre)
        if save:
            s["s3"][...] = gelu_slope(pre, cdf)
        store3(x4, 1, pre * cdf, Wh)

    block_three("pt", s["x3t"], s["x4t"], False)
    send("3t", *edges(s["x4t"], C2, Rh, Wh))
    block_three("pd", s["x3d"], s["x4d"], True)
    send("3d", *edges(s["x4d"], C2, Rh, Wh))
    for a in range(3):
        for b in range(3):
            w4t[a, :, b * C2 : (b + 1) * C2] = w4_raw[2 - a, 2 - b].T
    halo("3t", s["x4t"], Rh, Wh)
    pre = conv(w4, s["x4t"], 0, Rh, Wh) + b4
    s["act4t"][...] = pre * cdf_of(pre)
    halo("3d", s["x4d"], Rh, Wh)
    pre = conv(w4, s["x4d"], 0, Rh, Wh) + b4
    cdf = cdf_of(pre)
    part, grad = lpips(pre * cdf, s["act4t"][...], lin2, float((H // 2) * Wh))
    s["lacc"][1:2, : Rh * Wh] = part
    store3(s["xg4"], 1, grad * gelu_slope(pre, cdf), Wh)
    send("g4", *edges(s["xg4"], C2, Rh, Wh))
    for a in range(3):
        for b in range(3):
            w2t[a, :, b * C1 : (b + 1) * C1] = w2_raw[2 - a, 2 - b].T
    spread(0, wo_raw, True)
    spread(1, w1_raw, True)
    w1b = few[1, :72, :C1].astype(BF16)
    wf = few[0].T[:CF, :72].astype(BF16)

    def g3_rows(row, count):
        g3 = conv(w4t, s["xg4"], row, count, Wh) * s["s3"][:, span(row, count, Wh)]
        store3(s["xg3"], row + 1, g3, Wh)

    g3_rows(1, Rh - 2)
    halo("g4", s["xg4"], Rh, Wh)
    g3_rows(0, 1)
    g3_rows(Rh - 1, 1)
    send("g3", *edges(s["xg3"], C2, Rh, Wh))

    def g2_rows(first, count):
        gpool = conv(w3t, s["xg3"], first, count, Wh)
        for i in range(count):
            wide = dot_split(gpool[:, i * Wh : (i + 1) * Wh], up_m)
            for j in range(2):
                row = 2 * (first + i) + j
                g2 = (s["gf1"][:, span(row, 1)] + wide) * s["s2"][:, span(row, 1)]
                store3(s["xg2"], row + 1, g2, W)

    g2_rows(1, Rh - 2)
    halo("g3", s["xg3"], Rh, Wh)
    g2_rows(0, 1)
    g2_rows(Rh - 1, 1)
    send("g2", *edges(s["xg2"], C1, R, W))

    def g1_row(i):
        g1 = conv(w2t, s["xg2"], i, 1, W) * s["s1"][:, span(i + 1, 1)]
        return g1.astype(BF16)

    pb[...] = jnp.zeros_like(pb)
    partials(w1b, g1_row, range(1, R - 1))
    halo("g2", s["xg2"], R, W)
    partials(w1b, g1_row, (0, R - 1))
    send("gd", pb[:, : 2 * W], pb[:, R * W :])

    bias_grad = jnp.zeros((8, 1), F32)
    wgrad = jnp.zeros((72, CF), F32)

    def weight_terms(i):
        return lax.dot_general(
            im72(s["gdec"], i, 1), feat[:, span(i, 1)], (((1,), (1,)), ((), ())),
            preferred_element_type=F32,
        )

    middle = rounded(pb[:, span(2, R - 2)] / scale)
    store24(s["gdec"], 2, middle)
    for i in range(2, R - 2):
        wgrad = wgrad + weight_terms(i)
    above, below = receive("gd")
    first_two = rounded((pb[:, span(0, 2)] + above) / scale)
    last_two = rounded((pb[:, span(R, 2)] + below) / scale)
    col = lax.broadcasted_iota(jnp.int32, (1, 2 * W), 1)
    first_two = first_two * jnp.where(col < W, keep_up, 1.0)
    last_two = last_two * jnp.where(col < W, 1.0, keep_dn)
    store24(s["gdec"], 0, first_two)
    store24(s["gdec"], R, last_two)
    for i in (0, 1, R - 2, R - 1):
        wgrad = wgrad + weight_terms(i)
    for own in (middle, first_two[:, W:], last_two[:, :W]):
        bias_grad = bias_grad + jnp.sum(own, 1, keepdims=True)
    loss = jnp.sum(jnp.sum(s["lacc"][...], 0, keepdims=True), 1, keepdims=True)

    def everyone(axis, me, size, slots, base):
        out = []
        for k in range(1, size):
            out.append(
                pltpu.make_async_remote_copy(
                    src_ref=slots.at[me], dst_ref=slots.at[me],
                    send_sem=all_send.at[base + k], recv_sem=all_recv.at[base + k],
                    device_id={axis: (me + k) % size}, device_id_type=pl.DeviceIdType.MESH,
                )
            )
        return out

    slot_r, slot_c = s["slot_r"], s["slot_c"]
    wg = s["wg"]
    wg[:72] = wgrad
    wg[72:80] = jnp.broadcast_to(bias_grad, (8, CF))
    for o in range(3):
        for tap in range(9):
            slot_r[me_r, o * 9 + 8 - tap] = wg[tap * 8 + o]
        slot_r[me_r, 27 + o] = wg[72 + o]
    slot_r[me_r, 30:32] = jnp.broadcast_to(loss, (2, CF))
    first = everyone("row", me_r, nrow, slot_r, 0)
    for c in first:
        c.start()
    for i in range(R // 2):
        fg_out[:, span(i, 1)] = dot(wf, im72(s["gdec"], i, 1)).astype(BF16)
    for c in first:
        c.wait()
    total = slot_r[0]
    for k in range(1, nrow):
        total = total + slot_r[k]
    slot_c[me_c] = total
    second = everyone("clip", me_c, nclip, slot_c, nrow)
    for c in second:
        c.start()
    for i in range(R // 2, R):
        fg_out[:, span(i, 1)] = dot(wf, im72(s["gdec"], i, 1)).astype(BF16)
    for c in second:
        c.wait()
    total = slot_c[0]
    for k in range(1, nclip):
        total = total + slot_c[k]
    red_out[...] = total


def local(
    features, out_weight, out_bias, targets, weight_one, bias_one, weight_two, bias_two,
    weight_three, bias_three, weight_four, bias_four, lin_one, lin_two,
):
    _, CF, R, W = features.shape
    C1, C2 = weight_two.shape[0], weight_four.shape[0]
    nrow, nclip = lax.axis_size("row"), lax.axis_size("clip")
    Wh, Rh = W // 2, R // 2
    operands = (
        features.reshape(CF, R * W), targets[0], out_weight.transpose(0, 2, 3, 1),
        weight_one.transpose(1, 2, 3, 0), weight_two.transpose(2, 3, 0, 1),
        weight_three.transpose(2, 3, 1, 0), weight_four.transpose(2, 3, 0, 1), out_bias,
        bias_one[None], bias_two[None], lin_one[None], bias_three[None], bias_four[None],
        lin_two[None],
    )
    V = pltpu.VMEM
    scratch = [
        V((24, (R + 4) * W), F32), V((24, (R + 4) * W), F32), V((8, (R + 2) * W), F32),
        V((3 * C1, (R + 2) * W), BF16), V((3 * C1, (R + 2) * W), BF16),
        V((3 * C1, (Rh + 2) * Wh), BF16), V((3 * C1, (Rh + 2) * Wh), BF16),
        V((3 * C2, (Rh + 2) * Wh), BF16), V((3 * C2, (Rh + 2) * Wh), BF16),
        V((3 * C2, (Rh + 2) * Wh), BF16), V((3 * C2, (Rh + 2) * Wh), BF16),
        V((3 * C1, (R + 2) * W), BF16),
        V((C1, R * W), F32), V((C2, Rh * Wh), F32), V((C1, R * W), F32),
        V((C1, (R + 2) * W), F32), V((C1, R * W), F32), V((C2, Rh * Wh), F32),
        V((24, (R + 2) * W), F32), V((8, 2 * W), F32),
        V((nrow, 32, CF), F32), V((nclip, 32, CF), F32),
        V((3, C1, 3 * C1), BF16), V((3, C1, 3 * C1), BF16), V((3, C2, 3 * C1), BF16),
        V((3, C1, 3 * C2), BF16), V((3, C2, 3 * C2), BF16), V((3, C2, 3 * C2), BF16),
        V((2, 128, max(CF, C1, 128)), F32), V((8, 128), F32), V((8, R * W), F32), V((80, CF), F32),
    ]
    shapes = message_shapes(C1, C2, W)
    for name in MESSAGES:
        scratch += [V(*shapes[name])] * 4
    D = pltpu.SemaphoreType.DMA
    scratch += [D((2 * len(MESSAGES),)), D((2 * len(MESSAGES),)), D((nrow + nclip,)), D((nrow + nclip,))]
    vmem = pl.BlockSpec(memory_space=pltpu.VMEM)
    fg, red = pl.pallas_call(
        functools.partial(kernel_body, (R, W, C1, C2, CF, nrow, nclip)),
        out_shape=(
            jax.ShapeDtypeStruct((CF, R * W), BF16),
            jax.ShapeDtypeStruct((32, CF), F32),
        ),
        in_specs=[vmem] * 7 + [pl.BlockSpec(memory_space=pltpu.SMEM)] + [vmem] * 6,
        out_specs=(vmem, vmem),
        scratch_shapes=scratch,
        name="lpips_step",
        compiler_params=pltpu.CompilerParams(
            collective_id=0, has_side_effects=True, vmem_limit_bytes=62 * 1024 * 1024
        ),
    )(*operands)
    feature_grad = fg.reshape(1, CF, R, W)
    weight_grad = red[:27].reshape(3, 3, 3, CF).transpose(0, 3, 1, 2)
    return (red[30, 0], feature_grad, weight_grad, red[27:30, 0])


def solution(mesh):
    placed = [P()] * 14
    placed[0] = placed[3] = P("clip", None, "row", None)
    return jax.shard_map(
        local,
        mesh=mesh,
        in_specs=tuple(placed),
        out_specs=(P(), P("clip", None, "row", None), P(), P()),
        check_vma=False,
    )
```

time: 210 us -> 49.4 us (0.24)
  starting transfers between devices: 75.1 us -> 0 us
  Pallas kernels: 0 us -> 42.2 us
  blocking collectives: 41.5 us -> 0 us
  matrix products: 32.7 us -> 0 us
  local copies, waits for them, and re-layouts: 32.1 us -> 6.35 us
  other arithmetic: 11.8 us -> 0 us
  waiting for transfers between devices: 10.5 us -> 0 us
  between operations: 4.34 us -> 0.64 us
    ppermute x28 -> x0, starting transfers between devices: 75.1 us -> none  [the longest x13 53.9 us: padded_2(): before = lax.ppermute(last, axis, up)]
    pallas_call x0 -> x1, Pallas kernels: none -> 42.2 us  [local(): pl.pallas_call(functools.partial(kernel_body, (R, W, C1, C2, CF, nrow, nc...]
    psum x1 -> x0, blocking collectives: 41.5 us -> none  [local(): lax.psum((part_one + part_two, weight_grad, bias_grad), ('clip', 'row'))]
    dot_general x141 -> x0, matrix products: 32.7 us -> none  [the longest x126 29.1 us: conv_valid(): jnp.dot(weight[:, :, row_shift, col_shift], piece.reshape(channels, row_c...]
    ppermute x28 -> x0, waiting for transfers between devices: 10.5 us -> none  [the longest x13 10.5 us: padded_2(): after = lax.ppermute(leading, axis, down)]
    unnamed x129 -> x4, local copies, waits for them, and re-layouts: 11.2 us -> 3.92 us
    slice x34 -> x2, local copies, waits for them, and re-layouts: 6.7 us -> 1.81 us  [local(): return (red[30, 0], feature_grad, weight_grad, red[27:30, 0])]
    reduce_sum x3 -> x0, other arithmetic: 4.58 us -> none  [the longest x2 2.52 us: lpips_layer(): jnp.sum(grad_unit * unit_dec, 1, keepdims=True)]
  transfers between devices with their start and end apart: 28 -> 0, of which waited for: 7 -> 0; matrix products, arithmetic and copies ran while one was open for 10% -> 0% of each run, Pallas kernels for 0% -> 0%
where the time goes in v1:
time: 49.4 us; the launch traced here: 49.1 us
  Pallas kernels  42.2 us (85%)
  local copies, waits for them, and re-layouts  6.35 us (13%)
  between operations  0.64 us (1%)
    pallas_call x1, Pallas kernels, local(): pl.pallas_call(functools.partial(kernel_body, (R, W, C1, C2, CF, nrow, nc...  42.2 us
    unnamed x4, local copies, waits for them, and re-layouts  3.92 us
    slice x2, local copies, waits for them, and re-layouts, local(): return (red[30, 0], feature_grad, weight_grad, red[27:30, 0])  1.81 us

profile of v1, /device:TPU:0, one launch (start us, length us, event | category | flops | bytes accessed | tf_op | source)
XLA Modules:
  0.0 49.1 jit_solution(13864243526915803046)
XLA Ops:
  0.6 2.0 %copy.18 = bf16[16,8,8,256]{3,1,2,0:T(8,128)(2,1)} copy(bf16[16,8,8,256]{3,2,1,0:T(8,128)(2,1)} %bitcast.22) | data formatting | bytes 1048576
  2.6 42.2 %lpips_step.1 = (bf16[128,2048]{1,0:T(8,128)(2,1)}, f32[32,128]{1,0:T(8,128)}) custom-call(bf16[128,2048]{1,0:T(8,128)(2,1)} %bitcast.21, bf16[3,8,256]{2,1,0:T(8,128)(2,1)} %bitcast.30, bf16[3,3,3,128]{3,2,1,0:T(4,128)(2,1)} %bitcast.31, bf16[3,3,3,64]{3,2,1,0:T(4,128)(2,1)} %bitcast.32, bf16[3,3,64,64]{3,2,1,0:T(8,128)(2,1)} %bitcast.26, ...), custom_call_target="tpu_custom_call" | custom-call | tf_op jit(solution)/shard_map/lpips_step/pallas_call | solution.py:492
  44.7 1.2 %slice.9 = f32[1,1]{1,0:T(1,128)} slice(f32[32,128]{1,0:T(8,128)} %get-tuple-element.6), slice={[30:31], [0:1]} | slice | bytes 8 | tf_op jit(solution)/shard_map/slice | solution.py:508
  45.9 0.0 copy-start
  45.9 2.0 %copy.19 = bf16[16,8,8,256]{3,2,1,0:T(8,128)(2,1)} copy(bf16[16,8,8,256]{3,1,2,0:T(8,128)(2,1)} %bitcast.24) | data formatting | bytes 1048576
  47.9 0.0 copy-done
  47.9 0.6 %slice_reduce_fusion = f32[3]{0:T(128)} fusion(f32[32,128]{1,0:T(8,128)S(1)} %copy-done), kind=kLoop, calls=%fused_computation | loop fusion | bytes 24 | tf_op jit(solution)/shard_map/slice | solution.py:508
  48.5 0.6 %reshape.19 = f32[3,3,3,128]{3,2,1,0:T(4,128)} reshape(f32[27,128]{1,0:T(8,128)S(1)} %bitcast.28) | data formatting | bytes 27648 | tf_op jit(solution)/shard_map/reshape | solution.py:507
Async XLA Ops:
  45.9 2.0 %copy-start = (f32[32,128]{1,0:T(8,128)S(1)}, f32[32,128]{1,0:T(8,128)}, u32[]{:S(2)}) copy-start(f32[32,128]{1,0:T(8,128)} %get-tuple-element.6) | copy-start | bytes 49156
